TPU v7x, 32 devices: a whole 2x2x4 slice. The times are simulated.
32 devices in a mesh: tm: 16 (over z, y, core), space: 2 (over x).
Axes of the slice: x: 2, y: 2, z: 4, core: 2. Of those that a mesh axis runs over, the one named last changes fastest.
Arguments:
- queries: bfloat16 [32, 64, 3072], P('tm', 'space'), may hold values from -44 to 44
- keys: bfloat16 [32, 64, 3072], P('tm', 'space'), may hold values from -4 to 4
- values: bfloat16 [32, 64, 3072], P('tm', 'space'), may hold values from -24 to 24
- span_of_frame: int32 [32], replicated, may hold values from 0 to 15, never falling along the last dimension, each value on 1 to 4 neighbouring positions
Outputs:
- attended: bfloat16 [32, 64, 3072], P('tm', 'space')
Inputs may be any that keep to these rules, and one draw needn't show every extreme that they name: `span_of_frame`: span indices never fall along the frames; each of the 16 spans holds 1 to 4 frames, and some span holds exactly 4.
All inputs are finite; a program needn't handle non-finite values.
Results may differ from a plain program's by a relative error of at most 0.005.
Values may be sent and summed in bfloat16 or wider, within the bound.
No kernel may reach another device: no remote copies, remote signals or barrier semaphores. Data moves between devices by JAX's collectives and lax.ppermute only.
A program may use at most 128 MiB of HBM per device.

v0:
```python
import jax
import jax.numpy as jnp
from jax import lax
from jax.sharding import PartitionSpec as P

HD = 128
FR_DEV = 2


def block_update(state, key_block, value_block, key_spans, query_rows, query_spans):
    running_max, total, weighted = state
    scores = jnp.einsum(
        "qhd,khd->qhk", query_rows, key_block, preferred_element_type=jnp.float32
    ) * HD ** (-0.5)
    visible = (key_spans[None, :] <= query_spans[:, None])[:, None, :]
    block_max = jnp.max(jnp.where(visible, scores, -1e30), axis=2)
    new_max = jnp.maximum(running_max, block_max)
    probs = jnp.where(visible, jnp.exp(scores - new_max[:, :, None]), 0.0)
    factor = jnp.exp(running_max - new_max)
    total = total * factor + jnp.sum(probs, axis=2)
    weighted = weighted * factor[:, :, None] + jnp.einsum(
        "qhk,khd->qhd", probs.astype(jnp.bfloat16), value_block, preferred_element_type=jnp.float32
    )
    return (new_max, total, weighted)


def absorb(state, key_frames, value_frames, frame_spans, query_rows, query_spans):
    spatial = key_frames.shape[1]
    heads_here = query_rows.shape[1]
    count = key_frames.shape[0] // FR_DEV
    key_blocks = key_frames.reshape(count, FR_DEV * spatial, heads_here, HD)
    value_blocks = value_frames.reshape(count, FR_DEV * spatial, heads_here, HD)
    span_rows = jnp.repeat(frame_spans, spatial).reshape(count, FR_DEV * spatial)

    def step(index, carry):
        key_block = key_blocks[index]
        value_block = value_blocks[index]
        row_spans = span_rows[index]
        return block_update(carry, key_block, value_block, row_spans, query_rows, query_spans)

    return lax.fori_loop(0, count, step, state)


def per_device(queries, keys, values, span_of_frame):
    local_q, local_k, local_v = (
        lax.all_to_all(queries, "space", split_axis=2, concat_axis=1, tiled=True),
        lax.all_to_all(keys, "space", split_axis=2, concat_axis=1, tiled=True),
        lax.all_to_all(values, "space", split_axis=2, concat_axis=1, tiled=True),
    )
    frames_here, spatial, width_here = local_q.shape
    heads_here = width_here // HD
    rows = frames_here * spatial
    query_rows = local_q.reshape(rows, heads_here, HD)
    position = lax.axis_index("tm")
    my_spans = lax.dynamic_slice_in_dim(span_of_frame, position * frames_here, frames_here)
    query_spans = jnp.repeat(my_spans, spatial)
    state = (
        jnp.full((rows, heads_here), -1e30, jnp.float32),
        jnp.zeros((rows, heads_here), jnp.float32),
        jnp.zeros((rows, heads_here, HD), jnp.float32),
    )
    state = absorb(
        state,
        lax.all_gather(local_k, "tm", axis=0, tiled=True),
        lax.all_gather(local_v, "tm", axis=0, tiled=True),
        span_of_frame,
        query_rows,
        query_spans,
    )
    running_max, total, weighted = state
    result = (
        (weighted / total[:, :, None])
        .astype(jnp.bfloat16)
        .reshape(frames_here, spatial, width_here)
    )
    return lax.all_to_all(result, "space", split_axis=1, concat_axis=2, tiled=True)


def solution(mesh):
    return jax.shard_map(
        per_device,
        mesh=mesh,
        in_specs=(P("tm", "space", None), P("tm", "space", None), P("tm", "space", None), P()),
        out_specs=P("tm", "space", None),
        check_vma=False,
    )
```

profile of v0, /device:TPU:1, one launch (start us, length us, event | category | flops | bytes accessed | tf_op | source)
XLA Modules:
  0.0 244.6 jit_solution(5360635925772005987)
XLA Ops:
  6.5 3.6 %copy.22 = bf16[2,32,3072]{1,0,2:T(2,128)(2,1)S(1)} copy(bf16[2,32,3072]{2,1,0:T(8,128)(2,1)} %param.7) | data formatting | bytes 786432 | tf_op args[1]
  10.2 1.6 reshape.54
  11.7 8.8 %all_to_all.69 = bf16[2,2,49152]{2,1,0:T(2,128)(2,1)S(1)} all-to-all(bf16[2,2,49152]{2,1,0:T(2,128)(2,1)S(1)} %reshape.54), channel_id=1, replica_groups=mesh['tm'=16,'space'=2] {'space'}, dimensions={0} | all-to-all | bytes 786432 | tf_op jit(solution)/shard_map/all_to_all | solution.py:47
  21.3 2.6 %copy.24 = bf16[2,2,32,1536]{3,2,1,0:T(8,128)(2,1)} copy(bf16[2,2,32,1536]{2,0,3,1:T(2,128)(2,1)S(1)} %bitcast.54) | data formatting | bytes 786432 | tf_op jit(solution)/shard_map/all_to_all | solution.py:47
  24.0 1.9 copy.27
  25.8 1.6 reshape.58
  27.4 7.1 %all_to_all.70 = bf16[2,2,49152]{2,1,0:T(2,128)(2,1)S(1)} all-to-all(bf16[2,2,49152]{2,1,0:T(2,128)(2,1)S(1)} %reshape.58), channel_id=1, replica_groups=mesh['tm'=16,'space'=2] {'space'}, dimensions={0} | all-to-all | bytes 786432 | tf_op jit(solution)/shard_map/all_to_all | solution.py:48
  35.3 2.6 %copy.29 = bf16[2,2,32,1536]{3,2,1,0:T(8,128)(2,1)} copy(bf16[2,2,32,1536]{2,0,3,1:T(2,128)(2,1)S(1)} %bitcast.55) | data formatting | bytes 786432 | tf_op jit(solution)/shard_map/all_to_all | solution.py:48
  37.9 1.9 copy.25
  39.8 2.2 reshape.56
  42.0 3.5 %all-to-all-start.1 = ((bf16[2,2,49152]{2,1,0:T(2,128)(2,1)}), bf16[2,2,49152]{2,1,0:T(2,128)(2,1)S(1)}, u32[]{:S(2)}, u32[]{:S(2)}) async-start(bf16[2,2,49152]{2,1,0:T(2,128)(2,1)} %reshape.56), calls=%async_computation.1 | async-start | bytes 786432 | tf_op jit(solution)/shard_map/all_to_all | solution.py:46
  45.9 4.7 %all-to-all-done.1 = bf16[2,2,49152]{2,1,0:T(2,128)(2,1)S(1)} async-done(((bf16[2,2,49152]{2,1,0:T(2,128)(2,1)}), bf16[2,2,49152]{2,1,0:T(2,128)(2,1)S(1)}, u32[]{:S(2)}, u32[]{:S(2)}) %all-to-all-start.1) | async-done | bytes 393248 | tf_op jit(solution)/shard_map/all_to_all | solution.py:46
  52.8 34.7 %all-gather.3.cloned.1.call-done = bf16[32,64,1536]{2,1,0:T(8,128)(2,1)} async-done(((bf16[2,64,1536]{2,1,0:T(8,128)(2,1)}), bf16[32,64,1536]{2,1,0:T(8,128)(2,1)}) %all-gather.3.cloned.1.call-update) | async-done | bytes 6291472 | tf_op jit(solution)/shard_map/all_gather | solution.py:64
  87.5 12.3 %reshape.49 = bf16[16,128,12,128]{3,2,1,0:T(8,128)(2,1)} reshape(bf16[32,64,1536]{2,1,0:T(8,128)(2,1)} %all-gather.3.cloned.1.call-done) | data formatting | bytes 12582912 | tf_op jit(solution)/shard_map/reshape | solution.py:31
  99.7 8.0 %copy.30 = bf16[16,128,12,128]{3,1,2,0:T(8,128)(2,1)} copy(bf16[16,128,12,128]{3,2,1,0:T(8,128)(2,1)} %reshape.49) | data formatting | bytes 12582912
  107.7 42.2 %all-gather.5.cloned.1.call-done = bf16[32,64,1536]{2,1,0:T(8,128)(2,1)} async-done(((bf16[2,64,1536]{2,1,0:T(8,128)(2,1)}), bf16[32,64,1536]{2,1,0:T(8,128)(2,1)}) %all-gather.5.cloned.1.call-update) | async-done | bytes 6291472 | tf_op jit(solution)/shard_map/all_gather | solution.py:65
  149.9 12.2 %reshape.51 = bf16[16,128,12,128]{3,2,1,0:T(8,128)(2,1)} reshape(bf16[32,64,1536]{2,1,0:T(8,128)(2,1)} %all-gather.5.cloned.1.call-done) | data formatting | bytes 12582912 | tf_op jit(solution)/shard_map/reshape | solution.py:32
  162.1 12.0 %copy.32 = bf16[16,128,12,128]{1,3,2,0:T(8,128)(2,1)} copy(bf16[16,128,12,128]{3,2,1,0:T(8,128)(2,1)} %reshape.51) | data formatting | bytes 12582912
  174.1 53.0 %while.18 = (s32[]{:T(128)}, f32[128,12]{0,1:T(8,128)S(1)}, f32[128,12]{0,1:T(8,128)S(1)}, f32[128,12,128]{0,2,1:T(8,128)S(1)}, s32[16,128]{1,0:T(8,128)S(1)}, /...) while((s32[]{:T(128)}, f32[128,12]{0,1:T(8,128)S(1)}, ...), condition=%wide.region_3.4_spmd.clone, body=%wide.region_0.3_spmd.clone.sunk | while | flops 103046656 | bytes 5280389 | solution.py:41
  192.6 1.4 fusion.33
  202.5 1.4 fusion.33
  212.4 1.4 fusion.33
  222.4 1.4 fusion.33
  228.2 8.7 %all_to_all.71 = bf16[2,64,1536]{2,0,1:T(2,128)(2,1)S(1)} all-to-all(bf16[2,64,1536]{2,0,1:T(2,128)(2,1)S(1)} %copy.34), channel_id=1, replica_groups=mesh['tm'=16,'space'=2] {'space'}, dimensions={1} | all-to-all | bytes 786432 | tf_op jit(solution)/shard_map/all_to_all | solution.py:76
  (184 shorter events, 52.1 us)
Async XLA Ops:
  6.5 17.4 %copy-start = (bf16[2,32,3072]{2,1,0:T(8,128)(2,1)S(1)}, bf16[2,32,3072]{2,1,0:T(8,128)(2,1)}, u32[]{:S(2)}) copy-start(bf16[2,32,3072]{2,1,0:T(8,128)(2,1)} %param.8) | copy-start | bytes 1179652
  6.5 80.9 %all-gather.3.cloned.1.call-start = ((), (), s32[]{:S(2)}) async-start(), calls=%async_computation.4 | async-start | bytes 6684672 | tf_op jit(solution)/shard_map/all_gather | solution.py:64
  20.5 17.4 %copy-start.1 = (bf16[2,32,3072]{2,1,0:T(8,128)(2,1)S(1)}, bf16[2,32,3072]{2,1,0:T(8,128)(2,1)}, u32[]{:S(2)}) copy-start(bf16[2,32,3072]{2,1,0:T(8,128)(2,1)} %param.6) | copy-start | bytes 1179652
  23.9 126.0 %all-gather.5.cloned.1.call-start = ((), (), s32[]{:S(2)}) async-start(), calls=%async_computation.5 | async-start | bytes 6684672 | tf_op jit(solution)/shard_map/all_gather | solution.py:65
  25.8 19.7 %copy-start.2 = (s32[32]{0:T(128)S(1)}, s32[32]{0:T(128)}, u32[]{:S(2)}) copy-start(s32[32]{0:T(128)} %param.9) | copy-start | bytes 388
  42.0 8.6 %all-to-all-start.1 = ((bf16[2,2,49152]{2,1,0:T(2,128)(2,1)}), bf16[2,2,49152]{2,1,0:T(2,128)(2,1)S(1)}, u32[]{:S(2)}, u32[]{:S(2)}) async-start(bf16[2,2,49152]{2,1,0:T(2,128)(2,1)} %reshape.56), calls=%async_computation.1 | async-start | bytes 786432 | tf_op jit(solution)/shard_map/all_to_all | solution.py:46
Sparse Core Ops, SparseCore 0:
  24.0 63.4 all-gather.2
  89.7 60.0 all-gather.4
where the time goes:
time: 248 us; the launch traced here: 245 us
  waiting for transfers between devices  81.6 us (33%)
  local copies, waits for them, and re-layouts  70.8 us (29%)
  matrix products  45.1 us (18%)
  blocking collectives  24.6 us (10%)
  between operations  13.6 us (5%)
  other arithmetic  4.15 us (2%)
  starting transfers between devices  3.51 us (1%)
    all_gather x1, waiting for transfers between devices, per_device(): lax.all_gather(local_v, 'tm', axis=0, tiled=True)  42.2 us
    unnamed x18, local copies, waits for them, and re-layouts  35.1 us
    all_gather x1, waiting for transfers between devices, per_device(): lax.all_gather(local_k, 'tm', axis=0, tiled=True)  34.7 us
    dot_general x16, matrix products, block_update(): jnp.einsum('qhk,khd->qhd', probs.astype(jnp.bfloat16), value_block, prefe...  22.7 us
    dot_general x16, matrix products, block_update(): jnp.einsum('qhd,khd->qhk', query_rows, key_block, preferred_element_type=...  22.4 us
    reshape x1, local copies, waits for them, and re-layouts, absorb(): key_blocks = key_frames.reshape(count, FR_DEV * spatial, heads_here, HD)  12.3 us
    reshape x1, local copies, waits for them, and re-layouts, absorb(): value_blocks = value_frames.reshape(count, FR_DEV * spatial, heads_here, HD)  12.2 us
    all_to_all x1, blocking collectives, per_device(): lax.all_to_all(keys, 'space', split_axis=2, concat_axis=1, tiled=True)  8.81 us
  transfers between devices with their start and end apart: 3, of which 3 were waited for; matrix products, arithmetic and copies ran while one was open for 14% of the time, Pallas kernels for 0%

commit v1 on v0

v1 whole, which is shorter than its diff:
```python
import functools
import math

import jax
import jax.numpy as jnp
from jax import lax
from jax.experimental import pallas as pl
from jax.experimental.pallas import tpu as pltpu
from jax.sharding import PartitionSpec as P

HD = 128
BLOCK = 256
VMEM = pl.BlockSpec(memory_space=pltpu.VMEM)
SMEM = pl.BlockSpec(memory_space=pltpu.SMEM)


def slots_of(heads, devices):
    return [head * devices // heads for head in range(heads)]


def pack_kernel(slots, q_ref, k_ref, v_ref, out_ref):
    rows = q_ref.shape[0]
    for head, slot in enumerate(slots):
        for place, ref in enumerate((q_ref, k_ref, v_ref)):
            out_ref[slot, place * rows : (place + 1) * rows, :] = ref[:, head * HD : (head + 1) * HD]


def unpack_kernel(slots, in_ref, out_ref):
    for head, slot in enumerate(slots):
        out_ref[:, head * HD : (head + 1) * HD] = in_ref[slot]


def attend_kernel(plan, span_ref, active_ref, x_ref, out_ref, score_ref, peak_ref, total_ref, sum_ref):
    sources, rows, spatial, group, per_frames = plan
    blocks = sources // group
    size = group * rows
    frames_dev = rows // spatial
    block_tms = max(1, group // per_frames)
    block_frames = block_tms * frames_dev
    scale = HD ** (-0.5) * math.log2(math.e)

    def first_frame(block):
        return (block * group) // per_frames * frames_dev

    def part(block, place):
        got = x_ref[pl.ds(block * group, group), place * rows : (place + 1) * rows, :]
        return got.reshape(size, HD)

    def spans_along(block, dimension, shape):
        at = lax.broadcasted_iota(jnp.int32, shape, dimension)
        local = (at // rows) // per_frames * frames_dev + (at % rows) // spatial
        base = first_frame(block)
        spans = jnp.full(shape, span_ref[base], jnp.int32)
        for frame in range(1, block_frames):
            spans = jnp.where(local == frame, span_ref[base + frame], spans)
        return spans

    def fold(values, op):
        got = values[:, :HD]
        for start in range(HD, values.shape[1], HD):
            got = op(got, values[:, start : start + HD])
        return got

    def scores_of(query, block):
        key = part(block, 1)
        return lax.dot_general(query, key, (((1,), (1,)), ((), ())), preferred_element_type=jnp.float32)

    def one_block(block, _):
        low = span_ref[first_frame(block)]
        high = span_ref[first_frame(block) + block_frames - 1]
        whole, seen = jnp.int32(0), jnp.int32(0)
        for other in range(blocks):
            start = first_frame(other)
            whole += (span_ref[start + block_frames - 1] <= low).astype(jnp.int32)
            seen += (span_ref[start] <= high).astype(jnp.int32)
        query = part(block, 0)
        peak_ref[...] = jnp.full_like(peak_ref, -jnp.inf)

        def plain(other, _):
            scores = scores_of(query, other)
            score_ref[other] = scores
            peak_ref[...] = jnp.maximum(peak_ref[...], fold(scores, jnp.maximum))
            return 0

        def masked(other, _):
            visible = spans_along(other, 1, (size, size)) <= spans_along(block, 0, (size, size))
            scores = jnp.where(visible, scores_of(query, other), -jnp.inf)
            score_ref[other] = scores
            peak_ref[...] = jnp.maximum(peak_ref[...], fold(scores, jnp.maximum))
            return 0

        lax.fori_loop(0, whole, plain, 0)
        lax.fori_loop(whole, seen, masked, 0)
        peak = jnp.max(peak_ref[...], axis=1, keepdims=True) * scale
        peak_ref[...] = jnp.broadcast_to(peak, peak_ref.shape)
        total_ref[...] = jnp.zeros_like(total_ref)
        sum_ref[...] = jnp.zeros_like(sum_ref)

        def weigh(other, _):
            peaks = jnp.concatenate([peak_ref[...]] * (size // HD), axis=1)
            probs = jnp.exp2(score_ref[other] * scale - peaks)
            total_ref[...] += fold(probs, jnp.add)
            sum_ref[...] += jnp.dot(probs.astype(jnp.bfloat16), part(other, 2), preferred_element_type=jnp.float32)
            return 0

        lax.fori_loop(0, seen, weigh, 0)
        total = jnp.sum(total_ref[...], axis=1, keepdims=True)
        result = (sum_ref[...] / total).astype(jnp.bfloat16)
        out_ref[pl.ds(block * group, group)] = result.reshape(group, rows, HD)
        return 0

    @pl.when(active_ref[0] == 1)
    def _():
        lax.fori_loop(0, blocks, one_block, 0)


def per_device(axes, sizes, queries, keys, values, span_of_frame):
    frames_here, spatial_here, width = queries.shape
    heads = width // HD
    rows = frames_here * spatial_here
    devices = math.prod(sizes)
    slots = slots_of(heads, devices)
    packed = pl.pallas_call(
        functools.partial(pack_kernel, slots),
        out_shape=jax.ShapeDtypeStruct((devices, 3 * rows, HD), jnp.bfloat16),
        in_specs=[VMEM] * 3,
        out_specs=VMEM,
    )(*(array.reshape(rows, width) for array in (queries, keys, values)))
    arrived = lax.all_to_all(packed, axes, split_axis=0, concat_axis=0, tiled=True)
    me = lax.axis_index(axes)
    active = functools.reduce(jnp.logical_or, [me == slot for slot in slots]).astype(jnp.int32)
    group = max(1, BLOCK // rows)
    size = group * rows
    plan = (devices, rows, spatial_here, group, sizes[1])
    result = pl.pallas_call(
        functools.partial(attend_kernel, plan),
        out_shape=jax.ShapeDtypeStruct((devices, rows, HD), jnp.bfloat16),
        in_specs=[SMEM, SMEM, VMEM],
        out_specs=VMEM,
        scratch_shapes=[
            pltpu.VMEM((devices // group, size, size), jnp.float32),
            pltpu.VMEM((size, HD), jnp.float32),
            pltpu.VMEM((size, HD), jnp.float32),
            pltpu.VMEM((size, HD), jnp.float32),
        ],
    )(span_of_frame, active.reshape(1), arrived)
    returned = lax.all_to_all(result, axes, split_axis=0, concat_axis=0, tiled=True)
    out = pl.pallas_call(
        functools.partial(unpack_kernel, slots),
        out_shape=jax.ShapeDtypeStruct((rows, width), jnp.bfloat16),
        in_specs=[VMEM],
        out_specs=VMEM,
    )(returned)
    return out.reshape(queries.shape)


def solution(mesh):
    axes = ("tm", "space")
    sizes = tuple(mesh.shape[axis] for axis in axes)
    return jax.shard_map(
        functools.partial(per_device, axes, sizes),
        mesh=mesh,
        in_specs=(P("tm", "space", None), P("tm", "space", None), P("tm", "space", None), P()),
        out_specs=P("tm", "space", None),
        check_vma=False,
    )
```

time: 248 us -> 88.9 us (0.36); the launches traced: 245 us -> 88.2 us
  local copies, waits for them, and re-layouts: 70.8 us -> 1.17 us
  waiting for transfers between devices: 81.6 us -> 36.3 us
  matrix products: 45.1 us -> 0 us
  Pallas kernels: 0 us -> 22.9 us
  between operations: 13.6 us -> 0.12 us
  other arithmetic: 4.15 us -> 0 us
  blocking collectives: 24.6 us -> 20.6 us
  starting transfers between devices: 3.51 us -> 7.08 us
    all_gather x2 -> x0, waiting for transfers between devices: 76.8 us -> none  [the longest x1 42.2 us: per_device(): lax.all_gather(local_v, 'tm', axis=0, tiled=True)]
    dot_general x32 -> x0, matrix products: 45.1 us -> none  [the longest x16 22.7 us: block_update(): jnp.einsum('qhk,khd->qhd', probs.astype(jnp.bfloat16), value_block, prefe...]
    unnamed x18 -> x2, local copies, waits for them, and re-layouts: 35.1 us -> 1.17 us
    all_to_all x1, waiting for transfers between devices: 4.74 us -> 36.3 us  [per_device(): lax.all_to_all(packed, axes, split_axis=0, concat_axis=0, tiled=True)]
    reshape x5 -> x0, local copies, waits for them, and re-layouts: 25.8 us -> none  [the longest x1 12.3 us: absorb(): key_blocks = key_frames.reshape(count, FR_DEV * spatial, heads_here, HD)]
    pallas_call x0 -> x3, Pallas kernels: none -> 22.9 us  [the longest x1 18.4 us: per_device(): pl.pallas_call(functools.partial(attend_kernel, plan), out_shape=jax.Shap...]
    all_to_all x5 -> x0, local copies, waits for them, and re-layouts: 6.99 us -> none  [the longest x1 2.59 us: per_device(): lax.all_to_all(values, 'space', split_axis=2, concat_axis=1, tiled=True)]
    all_to_all x3 -> x1, blocking collectives: 24.6 us -> 20.6 us  [per_device(): lax.all_to_all(result, axes, split_axis=0, concat_axis=0, tiled=True)]
  transfers between devices with their start and end apart: 3 -> 1, of which waited for: 3 -> 1; matrix products, arithmetic and copies ran while one was open for 14% -> 0% of each run, Pallas kernels for 0% -> 0%
where the time goes in v1:
time: 88.9 us; the launch traced here: 88.2 us
  waiting for transfers between devices  36.3 us (41%)
  Pallas kernels  22.9 us (26%)
  blocking collectives  20.6 us (23%)
  starting transfers between devices  7.08 us (8%)
  local copies, waits for them, and re-layouts  1.17 us (1%)
    all_to_all x1, waiting for transfers between devices, per_device(): lax.all_to_all(packed, axes, split_axis=0, concat_axis=0, tiled=True)  36.3 us
    all_to_all x1, blocking collectives, per_device(): lax.all_to_all(result, axes, split_axis=0, concat_axis=0, tiled=True)  20.6 us
    pallas_call x1, Pallas kernels, per_device(): pl.pallas_call(functools.partial(attend_kernel, plan), out_shape=jax.Shap...  18.4 us
    all_to_all x1, starting transfers between devices, per_device(): lax.all_to_all(packed, axes, split_axis=0, concat_axis=0, tiled=True)  7.08 us
    pallas_call x1, Pallas kernels, per_device(): pl.pallas_call(functools.partial(pack_kernel, slots), out_shape=jax.Shape...  2.61 us
    pallas_call x1, Pallas kernels, per_device(): pl.pallas_call(functools.partial(unpack_kernel, slots), out_shape=jax.Sha...  1.86 us
  transfers between devices with their start and end apart: 1, of which 1 were waited for; matrix products, arithmetic and copies ran while one was open for 0% of the time, Pallas kernels for 0%

profile of v1, /device:TPU:1, one launch (start us, length us, event | category | flops | bytes accessed | tf_op | source)
XLA Modules:
  0.0 88.2 jit_solution(17923386365114267182)
XLA Ops:
  0.0 2.6 %shard_map.46 = bf16[32,192,128]{2,1,0:T(8,128)(2,1)} custom-call(bf16[64,3072]{1,0:T(8,128)(2,1)} %bitcast.5, bf16[64,3072]{1,0:T(8,128)(2,1)} %bitcast.6, bf16[64,3072]{1,0:T(8,128)(2,1)} %bitcast.7), custom_call_target="tpu_custom_call" | custom-call | tf_op jit(solution)/shard_map/pallas_call | solution.py:123
  2.6 7.1 %all-to-all-start = ((bf16[32,192,128]{2,1,0:T(8,128)(2,1)}), bf16[32,192,128]{2,1,0:T(8,128)(2,1)S(1)}, u32[]{:S(2)}, u32[]{:S(2)}) async-start(bf16[32,192,128]{2,1,0:T(8,128)(2,1)} %shard_map.46), calls=%async_computation | async-start | bytes 3145728 | tf_op jit(solution)/shard_map/all_to_all | solution.py:129
  9.8 36.3 %all-to-all-done.x_ref = bf16[32,192,128]{2,1,0:T(8,128)(2,1)S(1)} async-done(((bf16[32,192,128]{2,1,0:T(8,128)(2,1)}), bf16[32,192,128]{2,1,0:T(8,128)(2,1)S(1)}, u32[]{:S(2)}, u32[]{:S(2)}) %all-to-all-start) | async-done | bytes 1572896 | tf_op jit(solution)/shard_map/all_to_all | solution.py:129
  46.1 0.0 copy-start
  46.1 1.2 %copy-done = bf16[32,192,128]{2,1,0:T(8,128)(2,1)} copy-done((bf16[32,192,128]{2,1,0:T(8,128)(2,1)}, bf16[32,192,128]{2,1,0:T(8,128)(2,1)S(1)}, u32[]{:S(2)}) %copy-start) | copy-done | bytes 1572888
  47.3 18.4 %shard_map.47 = bf16[32,64,128]{2,1,0:T(8,128)(2,1)} custom-call(s32[32]{0:T(128)} %span_ref.1, s32[1]{0:T(128)} %bitcast.active_ref, bf16[32,192,128]{2,1,0:T(8,128)(2,1)} %copy-done), custom_call_target="tpu_custom_call" | custom-call | tf_op jit(solution)/shard_map/pallas_call | solution.py:135
  65.7 20.6 %all_to_all.10.in_ref = bf16[32,64,128]{2,1,0:T(8,128)(2,1)} all-to-all(bf16[32,64,128]{2,1,0:T(8,128)(2,1)} %shard_map.47), channel_id=1, replica_groups=mesh['tm'=16,'space'=2] {'tm','space'}, dimensions={0} | all-to-all | bytes 1048576 | tf_op jit(solution)/shard_map/all_to_all | solution.py:147
  86.3 1.9 %shard_map.48 = bf16[64,3072]{1,0:T(8,128)(2,1)} custom-call(bf16[32,64,128]{2,1,0:T(8,128)(2,1)} %all_to_all.10.in_ref), custom_call_target="tpu_custom_call" | custom-call | tf_op jit(solution)/shard_map/pallas_call | solution.py:148
Async XLA Ops:
  2.6 43.5 %all-to-all-start = ((bf16[32,192,128]{2,1,0:T(8,128)(2,1)}), bf16[32,192,128]{2,1,0:T(8,128)(2,1)S(1)}, u32[]{:S(2)}, u32[]{:S(2)}) async-start(bf16[32,192,128]{2,1,0:T(8,128)(2,1)} %shard_map.46), calls=%async_computation | async-start | bytes 3145728 | tf_op jit(solution)/shard_map/all_to_all | solution.py:129
  46.1 1.2 %copy-start = (bf16[32,192,128]{2,1,0:T(8,128)(2,1)}, bf16[32,192,128]{2,1,0:T(8,128)(2,1)S(1)}, u32[]{:S(2)}) copy-start(bf16[32,192,128]{2,1,0:T(8,128)(2,1)S(1)} %all-to-all-done.x_ref) | copy-start | bytes 4718596

commit v2 on v1

--- a/solution.py
+++ b/solution.py
@@ -114,7 +114,145 @@
         lax.fori_loop(0, blocks, one_block, 0)
 
 
+def unrolled_kernel(plan, span_ref, active_ref, x_ref, out_ref, score_ref, peak_ref, total_ref, sum_ref):
+    sources, rows, spatial, group, per_frames = plan
+    blocks = sources // group
+    size = group * rows
+    frames_dev = rows // spatial
+    block_frames = max(1, group // per_frames) * frames_dev
+    scale = HD ** (-0.5) * math.log2(math.e)
+
+    def first_frame(block):
+        return (block * group) // per_frames * frames_dev
+
+    def part(block, place):
+        return x_ref[pl.ds(block * group, group), place * rows : (place + 1) * rows, :].reshape(size, HD)
+
+    def spans_along(block, dimension, shape):
+        at = lax.broadcasted_iota(jnp.int32, shape, dimension)
+        local = (at // rows) // per_frames * frames_dev + (at % rows) // spatial
+        base = first_frame(block)
+        spans = jnp.full(shape, span_ref[base], jnp.int32)
+        for frame in range(1, block_frames):
+            spans = jnp.where(local == frame, span_ref[base + frame], spans)
+        return spans
+
+    def fold(values, op):
+        got = values[:, :HD]
+        for start in range(HD, values.shape[1], HD):
+            got = op(got, values[:, start : start + HD])
+        return got
+
+    def scores_of(query, key):
+        return lax.dot_general(query, key, (((1,), (1,)), ((), ())), preferred_element_type=jnp.float32)
+
+    def one_block(block):
+        high = span_ref[first_frame(block) + block_frames - 1]
+        seen = jnp.int32(block + 1)
+        for other in range(block + 1, blocks):
+            seen += (span_ref[first_frame(other)] <= high).astype(jnp.int32)
+        query = part(block, 0)
+
+        def masked(other):
+            visible = spans_along(other, 1, (1, size)) <= spans_along(block, 0, (size, 1))
+            return jnp.where(visible, scores_of(query, part(other, 1)), -jnp.inf)
+
+        scores = masked(block)
+        score_ref[block] = scores
+        top = fold(scores, jnp.maximum)
+        for other in range(block):
+            scores = scores_of(query, part(other, 1))
+            score_ref[other] = scores
+            top = jnp.maximum(top, fold(scores, jnp.maximum))
+        peak_ref[...] = top
+
+        def ahead(other, _):
+            scores = masked(other)
+            score_ref[other] = scores
+            peak_ref[...] = jnp.maximum(peak_ref[...], fold(scores, jnp.maximum))
+            return 0
+
+        lax.fori_loop(block + 1, seen, ahead, 0)
+        peak = jnp.max(peak_ref[...], axis=1, keepdims=True) * scale
+
+        def weigh(other):
+            probs = jnp.exp2(score_ref[other] * scale - peak)
+            weighed = jnp.dot(probs.astype(jnp.bfloat16), part(other, 2), preferred_element_type=jnp.float32)
+            return fold(probs, jnp.add), weighed
+
+        total, weighed = weigh(0)
+        for other in range(1, block + 1):
+            more_total, more = weigh(other)
+            total, weighed = total + more_total, weighed + more
+        total_ref[...], sum_ref[...] = total, weighed
+
+        def ahead_weigh(other, _):
+            more_total, more = weigh(other)
+            total_ref[...] += more_total
+            sum_ref[...] += more
+            return 0
+
+        lax.fori_loop(block + 1, seen, ahead_weigh, 0)
+        total = jnp.sum(total_ref[...], axis=1, keepdims=True)
+        result = (sum_ref[...] / total).astype(jnp.bfloat16)
+        out_ref[block * group : (block + 1) * group] = result.reshape(group, rows, HD)
+
+    @pl.when(active_ref[0] == 1)
+    def _():
+        for block in range(blocks):
+            one_block(block)
+
+
+def on_chip(axes, sizes, queries, keys, values, span_of_frame):
+    frames_here, spatial_here, width = queries.shape
+    heads = width // HD
+    rows = frames_here * spatial_here
+    devices = math.prod(sizes)
+    slots = slots_of(heads, devices)
+    me = lax.axis_index(axes)
+    active = functools.reduce(jnp.logical_or, [me == slot for slot in slots]).astype(jnp.int32)
+    local, active = lax.optimization_barrier(
+        ([array.reshape(rows, width) for array in (queries, keys, values)], active.reshape(1))
+    )
+    packed = pl.pallas_call(
+        functools.partial(pack_kernel, slots),
+        out_shape=pltpu.VMEM((devices, 3 * rows, HD), jnp.bfloat16),
+        in_specs=[VMEM] * 3,
+        out_specs=VMEM,
+    )(*local)
+    arrived = lax.all_to_all(packed, axes, split_axis=0, concat_axis=0, tiled=True)
+    group = max(1, BLOCK // rows)
+    size = group * rows
+    plan = (devices, rows, spatial_here, group, sizes[1])
+    result = pl.pallas_call(
+        functools.partial(unrolled_kernel, plan),
+        out_shape=pltpu.VMEM((devices, rows, HD), jnp.bfloat16),
+        in_specs=[SMEM, SMEM, VMEM],
+        out_specs=VMEM,
+        scratch_shapes=[
+            pltpu.VMEM((devices // group, size, size), jnp.float32),
+            pltpu.VMEM((size, HD), jnp.float32),
+            pltpu.VMEM((size, HD), jnp.float32),
+            pltpu.VMEM((size, HD), jnp.float32),
+        ],
+    )(span_of_frame, active, pltpu.with_memory_space_constraint(arrived, pltpu.VMEM))
+    returned = lax.all_to_all(result, axes, split_axis=0, concat_axis=0, tiled=True)
+    out = pl.pallas_call(
+        functools.partial(unpack_kernel, slots),
+        out_shape=jax.ShapeDtypeStruct((rows, width), jnp.bfloat16),
+        in_specs=[VMEM],
+        out_specs=VMEM,
+    )(pltpu.with_memory_space_constraint(returned, pltpu.VMEM))
+    return out.reshape(queries.shape)
+
+
 def per_device(axes, sizes, queries, keys, values, span_of_frame):
+    tokens = math.prod(sizes) * queries.shape[0] * queries.shape[1]
+    way = on_chip if tokens <= 16 * BLOCK else general
+    return way(axes, sizes, queries, keys, values, span_of_frame)
+
+
+def general(axes, sizes, queries, keys, values, span_of_frame):
     frames_here, spatial_here, width = queries.shape
     heads = width // HD
     rows = frames_here * spatial_here

time: 88.9 us -> 74.5 us (0.84)
  blocking collectives: 20.6 us -> 63.7 us
  waiting for transfers between devices: 36.3 us -> 0 us
  Pallas kernels: 22.9 us -> 10.5 us
  starting transfers between devices: 7.08 us -> 0 us
  local copies, waits for them, and re-layouts: 1.17 us -> 0 us
    all_to_all x1 -> x2, blocking collectives: 20.6 us -> 63.7 us  [the longest x1 45.2 us: on_chip(): lax.all_to_all(packed, axes, split_axis=0, concat_axis=0, tiled=True)]
    all_to_all x1 -> x0, waiting for transfers between devices: 36.3 us -> none  [per_device(): lax.all_to_all(packed, axes, split_axis=0, concat_axis=0, tiled=True)]
    pallas_call x3, Pallas kernels: 22.9 us -> 10.5 us  [the longest x1 8.24 us: on_chip(): pl.pallas_call(functools.partial(unrolled_kernel, plan), out_shape=pltpu....]
    all_to_all x1 -> x0, starting transfers between devices: 7.08 us -> none  [per_device(): lax.all_to_all(packed, axes, split_axis=0, concat_axis=0, tiled=True)]
    unnamed x2 -> x0, local copies, waits for them, and re-layouts: 1.17 us -> none
  transfers between devices with their start and end apart: 1 -> 0, of which waited for: 1 -> 0; matrix products, arithmetic and copies ran while one was open for 0% -> 0% of each run, Pallas kernels for 0% -> 0%
where the time goes in v2:
time: 74.5 us; the launch traced here: 74.2 us
  blocking collectives  63.7 us (86%)
  Pallas kernels  10.5 us (14%)
    all_to_all x1, blocking collectives, on_chip(): lax.all_to_all(packed, axes, split_axis=0, concat_axis=0, tiled=True)  45.2 us
    all_to_all x1, blocking collectives, on_chip(): lax.all_to_all(result, axes, split_axis=0, concat_axis=0, tiled=True)  18.4 us
    pallas_call x1, Pallas kernels, on_chip(): pl.pallas_call(functools.partial(unrolled_kernel, plan), out_shape=pltpu....  8.24 us

profile of v2, /device:TPU:1, one launch (start us, length us, event | category | flops | bytes accessed | tf_op | source)
XLA Modules:
  0.0 74.2 jit_solution(1502073400358268539)
XLA Ops:
  0.0 1.4 %shard_map.46 = bf16[32,192,128]{2,1,0:T(8,128)(2,1)S(1)} custom-call(bf16[64,3072]{1,0:T(8,128)(2,1)} %bitcast.5, bf16[64,3072]{1,0:T(8,128)(2,1)} %bitcast.6, bf16[64,3072]{1,0:T(8,128)(2,1)} %bitcast.7), custom_call_target="tpu_custom_call" | custom-call | tf_op jit(solution)/shard_map/pallas_call | solution.py:217
  1.4 45.2 %all_to_all.10.x_ref = bf16[32,192,128]{2,1,0:T(8,128)(2,1)S(1)} all-to-all(bf16[32,192,128]{2,1,0:T(8,128)(2,1)S(1)} %shard_map.46), channel_id=1, replica_groups=mesh['tm'=16,'space'=2] {'tm','space'}, dimensions={0} | all-to-all | bytes 3145728 | tf_op jit(solution)/shard_map/all_to_all | solution.py:223
  46.7 8.2 %shard_map.47 = bf16[32,64,128]{2,1,0:T(8,128)(2,1)S(1)} custom-call(s32[32]{0:T(128)} %span_ref.1, s32[1]{0:T(128)} %bitcast.3.active_ref, bf16[32,192,128]{2,1,0:T(8,128)(2,1)S(1)} %all_to_all.10.x_ref), custom_call_target="tpu_custom_call" | custom-call | tf_op jit(solution)/shard_map/pallas_call | solution.py:227
  54.9 18.4 %all_to_all.11.in_ref = bf16[32,64,128]{2,1,0:T(8,128)(2,1)S(1)} all-to-all(bf16[32,64,128]{2,1,0:T(8,128)(2,1)S(1)} %shard_map.47), channel_id=1, replica_groups=mesh['tm'=16,'space'=2] {'tm','space'}, dimensions={0} | all-to-all | bytes 1048576 | tf_op jit(solution)/shard_map/all_to_all | solution.py:239
  73.3 0.8 %shard_map.48 = bf16[64,3072]{1,0:T(8,128)(2,1)} custom-call(bf16[32,64,128]{2,1,0:T(8,128)(2,1)S(1)} %all_to_all.11.in_ref), custom_call_target="tpu_custom_call" | custom-call | tf_op jit(solution)/shard_map/pallas_call | solution.py:240

commit v3 on v1

--- a/solution.py
+++ b/solution.py
@@ -30,7 +30,7 @@
         out_ref[:, head * HD : (head + 1) * HD] = in_ref[slot]
 
 
-def attend_kernel(plan, span_ref, active_ref, x_ref, out_ref, score_ref, peak_ref, total_ref, sum_ref):
+def attend_loops(plan, span_ref, x_ref, out_ref, score_ref, peak_ref, total_ref, sum_ref):
     sources, rows, spatial, group, per_frames = plan
     blocks = sources // group
     size = group * rows
@@ -109,12 +109,146 @@
         out_ref[pl.ds(block * group, group)] = result.reshape(group, rows, HD)
         return 0
 
+    lax.fori_loop(0, blocks, one_block, 0)
+
+
+def attend_kernel(plan, span_ref, active_ref, *refs):
     @pl.when(active_ref[0] == 1)
     def _():
-        lax.fori_loop(0, blocks, one_block, 0)
+        attend_loops(plan, span_ref, *refs)
+
+
+def straight_kernel(plan, span_ref, active_ref, x_ref, out_ref, score_ref, peak_ref, total_ref, sum_ref):
+    sources, rows, spatial, group, per_frames = plan
+    blocks = sources // group
+    size = group * rows
+    frames_dev = rows // spatial
+    block_frames = max(1, group // per_frames) * frames_dev
+    scale = HD ** (-0.5) * math.log2(math.e)
+
+    def first_frame(block):
+        return (block * group) // per_frames * frames_dev
+
+    def local_frame(row):
+        return (row // rows) // per_frames * frames_dev + (row % rows) // spatial
+
+    def part(block, place):
+        return x_ref[block * group : (block + 1) * group, place * rows : (place + 1) * rows, :].reshape(size, HD)
+
+    def fold(values, op):
+        got = values[:, :HD]
+        for start in range(HD, values.shape[1], HD):
+            got = op(got, values[:, start : start + HD])
+        return got
+
+    def masked(scores, block, other):
+        local = local_frame(lax.broadcasted_iota(jnp.int32, (1, size), 1))
+        spans = jnp.full((1, size), span_ref[first_frame(other)], jnp.int32)
+        for frame in range(1, block_frames):
+            spans = jnp.where(local == frame, span_ref[first_frame(other) + frame], spans)
+        pieces = []
+        for start in range(0, size, spatial):
+            mine = span_ref[first_frame(block) + local_frame(start)]
+            pieces.append(jnp.where(spans <= mine, scores[start : start + spatial], -jnp.inf))
+        return jnp.concatenate(pieces, axis=0)
+
+    def seen(block):
+        return range(min(block + 2, blocks))
+
+    def make_scores(block):
+        query, top = part(block, 0), None
+        for other in seen(block):
+            scores = lax.dot_general(
+                query, part(other, 1), (((1,), (1,)), ((), ())), preferred_element_type=jnp.float32
+            )
+            if other >= block:
+                scores = masked(scores, block, other)
+            score_ref[block % 2, other] = scores
+            folded = fold(scores, jnp.maximum)
+            top = folded if top is None else jnp.maximum(top, folded)
+        return jnp.max(top, axis=1, keepdims=True) * scale
+
+    def weigh(block, peak):
+        total = weighed = None
+        for other in seen(block):
+            probs = jnp.exp2(score_ref[block % 2, other] * scale - peak)
+            folded = fold(probs, jnp.add)
+            product = jnp.dot(probs.astype(jnp.bfloat16), part(other, 2), preferred_element_type=jnp.float32)
+            total = folded if total is None else total + folded
+            weighed = product if weighed is None else weighed + product
+        result = weighed / jnp.sum(total, axis=1, keepdims=True)
+        out_ref[block * group : (block + 1) * group] = result.astype(jnp.bfloat16).reshape(group, rows, HD)
+
+    near = jnp.bool_(True)
+    for block in range(blocks - 2):
+        last = first_frame(block) + block_frames - 1
+        near = near & (span_ref[first_frame(block + 2)] > span_ref[last])
+    active = active_ref[0] == 1
+
+    @pl.when(active & near)
+    def _():
+        peak = make_scores(0)
+        for block in range(1, blocks):
+            following = make_scores(block)
+            weigh(block - 1, peak)
+            peak = following
+        weigh(blocks - 1, peak)
+
+    @pl.when(active & jnp.logical_not(near))
+    def _():
+        attend_loops(plan, span_ref, x_ref, out_ref, score_ref.at[0], peak_ref, total_ref, sum_ref)
+
+
+def on_chip(axes, sizes, queries, keys, values, span_of_frame):
+    frames_here, spatial_here, width = queries.shape
+    heads = width // HD
+    rows = frames_here * spatial_here
+    devices = math.prod(sizes)
+    slots = slots_of(heads, devices)
+    me = lax.axis_index(axes)
+    active = functools.reduce(jnp.logical_or, [me == slot for slot in slots]).astype(jnp.int32)
+    local, active = lax.optimization_barrier(
+        ([array.reshape(rows, width) for array in (queries, keys, values)], active.reshape(1))
+    )
+    packed = pl.pallas_call(
+        functools.partial(pack_kernel, slots),
+        out_shape=pltpu.VMEM((devices, 3 * rows, HD), jnp.bfloat16),
+        in_specs=[VMEM] * 3,
+        out_specs=VMEM,
+    )(*local)
+    arrived = lax.all_to_all(packed, axes, split_axis=0, concat_axis=0, tiled=True)
+    group = max(1, BLOCK // rows)
+    size = group * rows
+    plan = (devices, rows, spatial_here, group, sizes[1])
+    result = pl.pallas_call(
+        functools.partial(straight_kernel, plan),
+        out_shape=pltpu.VMEM((devices, rows, HD), jnp.bfloat16),
+        in_specs=[SMEM, SMEM, VMEM],
+        out_specs=VMEM,
+        scratch_shapes=[
+            pltpu.VMEM((2, devices // group, size, size), jnp.float32),
+            pltpu.VMEM((size, HD), jnp.float32),
+            pltpu.VMEM((size, HD), jnp.float32),
+            pltpu.VMEM((size, HD), jnp.float32),
+        ],
+    )(span_of_frame, active, pltpu.with_memory_space_constraint(arrived, pltpu.VMEM))
+    returned = lax.all_to_all(result, axes, split_axis=0, concat_axis=0, tiled=True)
+    out = pl.pallas_call(
+        functools.partial(unpack_kernel, slots),
+        out_shape=jax.ShapeDtypeStruct((rows, width), jnp.bfloat16),
+        in_specs=[VMEM],
+        out_specs=VMEM,
+    )(pltpu.with_memory_space_constraint(returned, pltpu.VMEM))
+    return out.reshape(queries.shape)
 
 
 def per_device(axes, sizes, queries, keys, values, span_of_frame):
+    tokens = math.prod(sizes) * queries.shape[0] * queries.shape[1]
+    way = on_chip if tokens <= 16 * BLOCK else general
+    return way(axes, sizes, queries, keys, values, span_of_frame)
+
+
+def general(axes, sizes, queries, keys, values, span_of_frame):
     frames_here, spatial_here, width = queries.shape
     heads = width // HD
     rows = frames_here * spatial_here

time: 88.9 us -> 71.1 us (0.80)
  blocking collectives: 20.6 us -> 63.7 us
  waiting for transfers between devices: 36.3 us -> 0 us
  Pallas kernels: 22.9 us -> 7.25 us
  starting transfers between devices: 7.08 us -> 0 us
  local copies, waits for them, and re-layouts: 1.17 us -> 0 us
    all_to_all x1 -> x2, blocking collectives: 20.6 us -> 63.7 us  [the longest x1 45.2 us: on_chip(): lax.all_to_all(packed, axes, split_axis=0, concat_axis=0, tiled=True)]
    all_to_all x1 -> x0, waiting for transfers between devices: 36.3 us -> none  [per_device(): lax.all_to_all(packed, axes, split_axis=0, concat_axis=0, tiled=True)]
    pallas_call x3, Pallas kernels: 22.9 us -> 7.25 us  [the longest x1 5 us: on_chip(): pl.pallas_call(functools.partial(straight_kernel, plan), out_shape=pltpu....]
    all_to_all x1 -> x0, starting transfers between devices: 7.08 us -> none  [per_device(): lax.all_to_all(packed, axes, split_axis=0, concat_axis=0, tiled=True)]
    unnamed x2 -> x0, local copies, waits for them, and re-layouts: 1.17 us -> none
  transfers between devices with their start and end apart: 1 -> 0, of which waited for: 1 -> 0; matrix products, arithmetic and copies ran while one was open for 0% -> 0% of each run, Pallas kernels for 0% -> 0%
where the time goes in v3:
time: 71.1 us; the launch traced here: 70.9 us
  blocking collectives  63.7 us (90%)
  Pallas kernels  7.25 us (10%)
    all_to_all x1, blocking collectives, on_chip(): lax.all_to_all(packed, axes, split_axis=0, concat_axis=0, tiled=True)  45.2 us
    all_to_all x1, blocking collectives, on_chip(): lax.all_to_all(result, axes, split_axis=0, concat_axis=0, tiled=True)  18.4 us
    pallas_call x1, Pallas kernels, on_chip(): pl.pallas_call(functools.partial(straight_kernel, plan), out_shape=pltpu....  5 us
    pallas_call x1, Pallas kernels, on_chip(): pl.pallas_call(functools.partial(pack_kernel, slots), out_shape=pltpu.VME...  1.44 us

profile of v3, /device:TPU:1, one launch (start us, length us, event | category | flops | bytes accessed | tf_op | source)
XLA Modules:
  0.0 70.9 jit_solution(1273014343602478995)
XLA Ops:
  0.0 1.4 %shard_map.46 = bf16[32,192,128]{2,1,0:T(8,128)(2,1)S(1)} custom-call(bf16[64,3072]{1,0:T(8,128)(2,1)} %bitcast.5, bf16[64,3072]{1,0:T(8,128)(2,1)} %bitcast.6, bf16[64,3072]{1,0:T(8,128)(2,1)} %bitcast.7), custom_call_target="tpu_custom_call" | custom-call | tf_op jit(solution)/shard_map/pallas_call | solution.py:213
  1.4 45.2 %all_to_all.10.x_ref = bf16[32,192,128]{2,1,0:T(8,128)(2,1)S(1)} all-to-all(bf16[32,192,128]{2,1,0:T(8,128)(2,1)S(1)} %shard_map.46), channel_id=1, replica_groups=mesh['tm'=16,'space'=2] {'tm','space'}, dimensions={0} | all-to-all | bytes 3145728 | tf_op jit(solution)/shard_map/all_to_all | solution.py:219
  46.7 5.0 %shard_map.47 = bf16[32,64,128]{2,1,0:T(8,128)(2,1)S(1)} custom-call(s32[32]{0:T(128)} %span_ref.1, s32[1]{0:T(128)} %bitcast.3.active_ref, bf16[32,192,128]{2,1,0:T(8,128)(2,1)S(1)} %all_to_all.10.x_ref), custom_call_target="tpu_custom_call" | custom-call | tf_op jit(solution)/shard_map/pallas_call | solution.py:223
  51.7 18.4 %all_to_all.11.in_ref = bf16[32,64,128]{2,1,0:T(8,128)(2,1)S(1)} all-to-all(bf16[32,64,128]{2,1,0:T(8,128)(2,1)S(1)} %shard_map.47), channel_id=1, replica_groups=mesh['tm'=16,'space'=2] {'tm','space'}, dimensions={0} | all-to-all | bytes 1048576 | tf_op jit(solution)/shard_map/all_to_all | solution.py:235
  70.1 0.8 %shard_map.48 = bf16[64,3072]{1,0:T(8,128)(2,1)} custom-call(bf16[32,64,128]{2,1,0:T(8,128)(2,1)S(1)} %all_to_all.11.in_ref), custom_call_target="tpu_custom_call" | custom-call | tf_op jit(solution)/shard_map/pallas_call | solution.py:236

commit v4 on v3

--- a/solution.py
+++ b/solution.py
@@ -242,9 +242,209 @@
     return out.reshape(queries.shape)
 
 
+def shared_pack_kernel(q_ref, k_ref, v_ref, out_ref):
+    rows = q_ref.shape[0]
+    half, kept = rows // 2, rows - rows // 4
+
+    def of(ref, head, start=0, stop=rows):
+        return ref[start:stop, head * HD : (head + 1) * HD]
+
+    for time in range(0, out_ref.shape[0] // 2, 2):
+        for place in range(2):
+            own, both = time // 2 * 3 + 2 * place, time // 2 * 3 + 1
+            for slot, head in ((time * 2 + place, own), (time * 2 + 2 + place, both)):
+                out_ref[slot, :rows] = of(k_ref, head)
+                out_ref[slot, rows : 2 * rows] = of(v_ref, head)
+            out_ref[time * 2 + place, 2 * rows :] = of(q_ref, own, 0, kept)
+            out_ref[time * 2 + 2 + place, 2 * rows : 2 * rows + half] = of(q_ref, both, place * half, (place + 1) * half)
+            out_ref[time * 2 + 2 + place, 2 * rows + half :] = of(q_ref, own, kept, rows)
+
+
+def shared_unpack_kernel(in_ref, out_ref):
+    rows = out_ref.shape[0]
+    half = rows // 2
+    for time in range(0, in_ref.shape[0] // 2, 2):
+        for place in range(2):
+            own, both = time // 2 * 3 + 2 * place, time // 2 * 3 + 1
+            out_ref[:, own * HD : (own + 1) * HD] = in_ref[time * 2 + place]
+            out_ref[place * half : (place + 1) * half, both * HD : (both + 1) * HD] = in_ref[time * 2 + 2 + place, :half]
+
+
+def shared_kernel(plan, span_ref, me_ref, x_ref, rest_ref, out_ref, score_ref, peak_ref, total_ref, sum_ref):
+    devices, rows, spatial, group = plan
+    blocks = devices // group
+    size = group * rows
+    half = rows // 2
+    block_frames = group // 2 * (rows // spatial)
+    scale = HD ** (-0.5) * math.log2(math.e)
+
+    def local_frame(row):
+        return row // (2 * rows) * (rows // spatial) + row % rows // spatial
+
+    def part(block, place):
+        got = x_ref[pl.ds(block * group, group), place * rows : (place + 1) * rows, :]
+        return got.reshape(size, HD)
+
+    def fold(values, op):
+        got = values[:, :HD]
+        for start in range(HD, values.shape[1], HD):
+            got = op(got, values[:, start : start + HD])
+        return got
+
+    def scores_of(query, other, mine):
+        key = part(other, 0)
+        scores = lax.dot_general(query, key, (((1,), (1,)), ((), ())), preferred_element_type=jnp.float32)
+        if mine is None:
+            return scores
+        local = local_frame(lax.broadcasted_iota(jnp.int32, (1, size), 1))
+        spans = jnp.full((1, size), span_ref[other * block_frames], jnp.int32)
+        for frame in range(1, block_frames):
+            spans = jnp.where(local == frame, span_ref[other * block_frames + frame], spans)
+        pieces = []
+        for start in range(0, size, spatial):
+            pieces.append(jnp.where(spans <= mine(start), scores[start : start + spatial], -jnp.inf))
+        return jnp.concatenate(pieces, axis=0)
+
+    def probs_of(slot, other, peak):
+        probs = jnp.exp2(score_ref[slot, other] * scale - peak)
+        product = jnp.dot(probs.astype(jnp.bfloat16), part(other, 1), preferred_element_type=jnp.float32)
+        return fold(probs, jnp.add), product
+
+    def straight(wide, query_of, mine_of, write):
+        tiles = blocks // wide
+
+        def seen(tile):
+            return range(min((tile + 1) * wide + 1, blocks))
+
+        def make_scores(tile):
+            query, top = query_of(tile), None
+            for other in seen(tile):
+                scores = scores_of(query, other, mine_of(tile) if other >= tile * wide else None)
+                score_ref[tile % 2, other] = scores
+                folded = fold(scores, jnp.maximum)
+                top = folded if top is None else jnp.maximum(top, folded)
+            return jnp.max(top, axis=1, keepdims=True) * scale
+
+        def weigh(tile, peak):
+            total = weighed = None
+            for other in seen(tile):
+                folded, product = probs_of(tile % 2, other, peak)
+                total = folded if total is None else total + folded
+                weighed = product if weighed is None else weighed + product
+            write(tile, (weighed / jnp.sum(total, axis=1, keepdims=True)).astype(jnp.bfloat16))
+
+        peak = make_scores(0)
+        for tile in range(1, tiles):
+            following = make_scores(tile)
+            weigh(tile - 1, peak)
+            peak = following
+        weigh(tiles - 1, peak)
+
+    def looped(wide, query_of, mine_of, write):
+        for tile in range(blocks // wide):
+            query, mine = query_of(tile), mine_of(tile)
+            peak_ref[...] = jnp.full_like(peak_ref, -jnp.inf)
+            total_ref[...] = jnp.zeros_like(total_ref)
+            sum_ref[...] = jnp.zeros_like(sum_ref)
+
+            def score(other, _, query=query, mine=mine):
+                scores = scores_of(query, other, mine)
+                score_ref[0, other] = scores
+                peak_ref[...] = jnp.maximum(peak_ref[...], fold(scores, jnp.maximum))
+                return 0
+
+            lax.fori_loop(0, blocks, score, 0)
+            peak = jnp.max(peak_ref[...], axis=1, keepdims=True) * scale
+
+            def weigh(other, _, peak=peak):
+                folded, product = probs_of(0, other, peak)
+                total_ref[...] += folded
+                sum_ref[...] += product
+                return 0
+
+            lax.fori_loop(0, blocks, weigh, 0)
+            write(tile, (sum_ref[...] / jnp.sum(total_ref[...], axis=1, keepdims=True)).astype(jnp.bfloat16))
+
+    def own_query(tile):
+        sources = pl.ds(tile * group, group)
+        return jnp.concatenate([x_ref[sources, 2 * rows :, :], rest_ref[sources]], axis=1).reshape(size, HD)
+
+    def own_span(tile):
+        return lambda start: span_ref[tile * block_frames + local_frame(start)]
+
+    def own_write(tile, result):
+        out_ref[pl.ds(tile * group, group)] = result.reshape(group, rows, HD)
+
+    def both_query(tile):
+        return x_ref[pl.ds(tile * 2 * group, 2 * group), 2 * rows : 2 * rows + half, :].reshape(size, HD)
+
+    def both_span(tile):
+        return lambda start: span_ref[(tile * 2 * group + start // half) // 2 * 2 + me_ref[1]]
+
+    def both_write(tile, result):
+        out_ref[pl.ds(tile * 2 * group, 2 * group), :half, :] = result.reshape(2 * group, half, HD)
+
+    near = jnp.bool_(True)
+    for block in range(blocks - 2):
+        near = near & (span_ref[(block + 2) * block_frames] > span_ref[(block + 1) * block_frames - 1])
+    for core, roles in enumerate(((1, own_query, own_span, own_write), (2, both_query, both_span, both_write))):
+        here = me_ref[0] == core
+        pl.when(here & near)(functools.partial(straight, *roles))
+        pl.when(here & jnp.logical_not(near))(functools.partial(looped, *roles))
+
+
+def shared(axes, sizes, queries, keys, values, span_of_frame):
+    frames_here, spatial_here, width = queries.shape
+    rows = frames_here * spatial_here
+    devices = math.prod(sizes)
+    group = BLOCK // rows
+    size = group * rows
+    me = jnp.stack([lax.axis_index(axes[0]) % 2, lax.axis_index(axes[1])]).astype(jnp.int32)
+    local, me = lax.optimization_barrier(([array.reshape(rows, width) for array in (queries, keys, values)], me))
+    kept = rows - rows // 4
+    packed = pl.pallas_call(
+        shared_pack_kernel,
+        out_shape=pltpu.VMEM((devices, 2 * rows + kept, HD), jnp.bfloat16),
+        in_specs=[VMEM] * 3,
+        out_specs=VMEM,
+    )(*local)
+    arrived = lax.all_to_all(packed, axes, split_axis=0, concat_axis=0, tiled=True)
+    across = [(device, device ^ sizes[1]) for device in range(devices)]
+    rest = lax.ppermute(arrived[:, 2 * rows + rows // 2 :], axes, across)
+    result = pl.pallas_call(
+        functools.partial(shared_kernel, (devices, rows, spatial_here, group)),
+        out_shape=pltpu.VMEM((devices, rows, HD), jnp.bfloat16),
+        in_specs=[SMEM, SMEM, VMEM, VMEM],
+        out_specs=VMEM,
+        scratch_shapes=[
+            pltpu.VMEM((2, devices // group, size, size), jnp.float32),
+            pltpu.VMEM((size, HD), jnp.float32),
+            pltpu.VMEM((size, HD), jnp.float32),
+            pltpu.VMEM((size, HD), jnp.float32),
+        ],
+    )(
+        span_of_frame,
+        me,
+        pltpu.with_memory_space_constraint(arrived, pltpu.VMEM),
+        pltpu.with_memory_space_constraint(rest, pltpu.VMEM),
+    )
+    returned = lax.all_to_all(result, axes, split_axis=0, concat_axis=0, tiled=True)
+    out = pl.pallas_call(
+        shared_unpack_kernel,
+        out_shape=jax.ShapeDtypeStruct((rows, width), jnp.bfloat16),
+        in_specs=[VMEM],
+        out_specs=VMEM,
+    )(pltpu.with_memory_space_constraint(returned, pltpu.VMEM))
+    return out.reshape(queries.shape)
+
+
 def per_device(axes, sizes, queries, keys, values, span_of_frame):
     tokens = math.prod(sizes) * queries.shape[0] * queries.shape[1]
     way = on_chip if tokens <= 16 * BLOCK else general
+    frames_here, spatial_here, width = queries.shape
+    fits = sizes[1] == 2 and sizes[0] % 2 == 0 and 2 * (width // HD) == 3 * sizes[0] and frames_here == 2
+    if way is on_chip and fits and spatial_here % 32 == 0 and BLOCK % (4 * spatial_here) == 0:
+        way = shared
     return way(axes, sizes, queries, keys, values, span_of_frame)
 
 

time: 71.1 us -> 70.4 us (level)
  Pallas kernels: 7.25 us -> 5.53 us
  waiting for transfers between devices: 0 us -> 1.33 us
  blocking collectives: 63.7 us -> 62.6 us
    pallas_call x3, Pallas kernels: 7.25 us -> 5.53 us  [the longest x1 3.26 us: shared(): pl.pallas_call(functools.partial(shared_kernel, (devices, rows, spatial_h...]
    ppermute x0 -> x1, waiting for transfers between devices: none -> 1.33 us  [shared(): rest = lax.ppermute(arrived[:, 2 * rows + rows // 2:], axes, across)]
    all_to_all x2, blocking collectives: 63.7 us -> 62.6 us  [the longest x1 42.5 us: shared(): lax.all_to_all(packed, axes, split_axis=0, concat_axis=0, tiled=True)]
  transfers between devices with their start and end apart: 0 -> 1, of which waited for: 0 -> 1; matrix products, arithmetic and copies ran while one was open for 0% -> 0% of each run, Pallas kernels for 0% -> 0%
where the time goes in v4:
time: 70.4 us; the launch traced here: 70.2 us
  blocking collectives  62.6 us (89%)
  Pallas kernels  5.53 us (8%)
  waiting for transfers between devices  1.33 us (2%)
    all_to_all x1, blocking collectives, shared(): lax.all_to_all(packed, axes, split_axis=0, concat_axis=0, tiled=True)  42.5 us
    all_to_all x1, blocking collectives, shared(): lax.all_to_all(result, axes, split_axis=0, concat_axis=0, tiled=True)  20.1 us
    pallas_call x1, Pallas kernels, shared(): pl.pallas_call(functools.partial(shared_kernel, (devices, rows, spatial_h...  3.26 us
    pallas_call x1, Pallas kernels, shared(): pl.pallas_call(shared_pack_kernel, out_shape=pltpu.VMEM((devices, 2 * row...  1.46 us
  transfers between devices with their start and end apart: 1, of which 1 were waited for; matrix products, arithmetic and copies ran while one was open for 0% of the time, Pallas kernels for 0%

profile of v4, /device:TPU:1, one launch (start us, length us, event | category | flops | bytes accessed | tf_op | source)
XLA Modules:
  0.0 70.2 jit_solution(15973561571686520197)
XLA Ops:
  0.0 0.6 pad_add_fusion.me_ref
  0.6 1.5 %shard_map.46 = bf16[32,176,128]{2,1,0:T(8,128)(2,1)S(1)} custom-call(bf16[64,3072]{1,0:T(8,128)(2,1)} %bitcast.6, bf16[64,3072]{1,0:T(8,128)(2,1)} %bitcast.7, bf16[64,3072]{1,0:T(8,128)(2,1)} %bitcast.8), custom_call_target="tpu_custom_call" | custom-call | tf_op jit(solution)/shard_map/pallas_call | solution.py:405
  2.1 42.5 %all_to_all.10.x_ref = bf16[32,176,128]{2,1,0:T(8,128)(2,1)S(1)} all-to-all(bf16[32,176,128]{2,1,0:T(8,128)(2,1)S(1)} %shard_map.46), channel_id=1, replica_groups=mesh['tm'=16,'space'=2] {'tm','space'}, dimensions={0} | all-to-all | bytes 2883584 | tf_op jit(solution)/shard_map/all_to_all | solution.py:411
  44.6 0.1 collective-permute-start
  44.7 1.3 %collective-permute-done.rest_ref = bf16[32,16,128]{2,1,0:T(8,128)(2,1)S(1)} collective-permute-done((bf16[32,16,128]{2,1,0:T(8,128)(2,1)S(1)}, bf16[32,16,128]{2,1,0:T(8,128)(2,1)S(1)}, u32[]{:S(2)}, u32[]{:S(2)}) %collective-permute-start) | collective-permute-done | bytes 131104 | tf_op jit(solution)/shard_map/ppermute | solution.py:413
  46.0 3.3 %shard_map.47 = bf16[32,64,128]{2,1,0:T(8,128)(2,1)S(1)} custom-call(s32[32]{0:T(128)} %span_ref.1, s32[2]{0:T(128)} %pad_add_fusion.me_ref, bf16[32,176,128]{2,1,0:T(8,128)(2,1)S(1)} %all_to_all.10.x_ref, bf16[32,16,128]{2,1,0:T(8,128)(2,1)S(1)} %collective-permute-done.rest_ref), custom_call_target="tpu_custom_call" | custom-call | tf_op jit(solution)/shard_map/pallas_call | solution.py:414
  49.3 20.1 %all_to_all.11.in_ref = bf16[32,64,128]{2,1,0:T(8,128)(2,1)S(1)} all-to-all(bf16[32,64,128]{2,1,0:T(8,128)(2,1)S(1)} %shard_map.47), channel_id=1, replica_groups=mesh['tm'=16,'space'=2] {'tm','space'}, dimensions={0} | all-to-all | bytes 1048576 | tf_op jit(solution)/shard_map/all_to_all | solution.py:431
  69.4 0.8 %shard_map.48 = bf16[64,3072]{1,0:T(8,128)(2,1)} custom-call(bf16[32,64,128]{2,1,0:T(8,128)(2,1)S(1)} %all_to_all.11.in_ref), custom_call_target="tpu_custom_call" | custom-call | tf_op jit(solution)/shard_map/pallas_call | solution.py:432
  (1 shorter events, 0.0 us)
Async XLA Ops:
  44.6 1.4 %collective-permute-start = (bf16[32,16,128]{2,1,0:T(8,128)(2,1)S(1)}, bf16[32,16,128]{2,1,0:T(8,128)(2,1)S(1)}, u32[]{:S(2)}, u32[]{:S(2)}) collective-permute-start(bf16[32,16,128]{2,1,0:T(8,128)(2,1)S(1)} %slice.4), channel_id=1, source_target_pairs={{0,2},{1,3},{2,0},{3,1},{4,6},{5,7},{6,4},{7,5},{8,10},{9,11},{10,... | collective-permute-start | bytes 393224 | tf_op jit(solution)/shard_map/ppermute | solution.py:413

commit v5 on v4

--- a/solution.py
+++ b/solution.py
@@ -242,22 +242,33 @@
     return out.reshape(queries.shape)
 
 
-def shared_pack_kernel(q_ref, k_ref, v_ref, out_ref):
+def shared_pack_kernel(q_ref, k_ref, v_ref, out_ref, local_ref, sems):
     rows = q_ref.shape[0]
     half, kept = rows // 2, rows - rows // 4
-
-    def of(ref, head, start=0, stop=rows):
-        return ref[start:stop, head * HD : (head + 1) * HD]
-
+    copies = [
+        pltpu.make_async_copy(ref, local_ref.at[index], sems.at[index]) for index, ref in enumerate((k_ref, v_ref, q_ref))
+    ]
+    for copy in copies:
+        copy.start()
+    slots = []
     for time in range(0, out_ref.shape[0] // 2, 2):
         for place in range(2):
             own, both = time // 2 * 3 + 2 * place, time // 2 * 3 + 1
-            for slot, head in ((time * 2 + place, own), (time * 2 + 2 + place, both)):
-                out_ref[slot, :rows] = of(k_ref, head)
-                out_ref[slot, rows : 2 * rows] = of(v_ref, head)
-            out_ref[time * 2 + place, 2 * rows :] = of(q_ref, own, 0, kept)
-            out_ref[time * 2 + 2 + place, 2 * rows : 2 * rows + half] = of(q_ref, both, place * half, (place + 1) * half)
-            out_ref[time * 2 + 2 + place, 2 * rows + half :] = of(q_ref, own, kept, rows)
+            slots.append((time * 2 + place, time * 2 + 2 + place, own, both, place))
+
+    def of(index, head, start=0, stop=rows):
+        return local_ref[index, start:stop, head * HD : (head + 1) * HD]
+
+    for index in range(2):
+        copies[index].wait()
+        for first, second, own, both, _ in slots:
+            out_ref[first, index * rows : (index + 1) * rows] = of(index, own)
+            out_ref[second, index * rows : (index + 1) * rows] = of(index, both)
+    copies[2].wait()
+    for first, second, own, both, place in slots:
+        out_ref[first, 2 * rows :] = of(2, own, 0, kept)
+        out_ref[second, 2 * rows : 2 * rows + half] = of(2, both, place * half, (place + 1) * half)
+        out_ref[second, 2 * rows + half :] = of(2, own, kept, rows)
 
 
 def shared_unpack_kernel(in_ref, out_ref):
@@ -270,8 +281,9 @@
             out_ref[place * half : (place + 1) * half, both * HD : (both + 1) * HD] = in_ref[time * 2 + 2 + place, :half]
 
 
-def shared_kernel(plan, span_ref, me_ref, x_ref, rest_ref, out_ref, score_ref, peak_ref, total_ref, sum_ref):
+def shared_kernel(plan, axes, span_ref, x_ref, rest_ref, out_ref, score_ref, peak_ref, total_ref, sum_ref):
     devices, rows, spatial, group = plan
+    my_core, my_place = lax.axis_index(axes[0]) % 2, lax.axis_index(axes[1])
     blocks = devices // group
     size = group * rows
     half = rows // 2
@@ -333,12 +345,12 @@
                 weighed = product if weighed is None else weighed + product
             write(tile, (weighed / jnp.sum(total, axis=1, keepdims=True)).astype(jnp.bfloat16))
 
-        peak = make_scores(0)
-        for tile in range(1, tiles):
+        peak = make_scores(tiles - 1)
+        for tile in range(tiles - 2, -1, -1):
             following = make_scores(tile)
-            weigh(tile - 1, peak)
+            weigh(tile + 1, peak)
             peak = following
-        weigh(tiles - 1, peak)
+        weigh(0, peak)
 
     def looped(wide, query_of, mine_of, write):
         for tile in range(blocks // wide):
@@ -379,7 +391,7 @@
         return x_ref[pl.ds(tile * 2 * group, 2 * group), 2 * rows : 2 * rows + half, :].reshape(size, HD)
 
     def both_span(tile):
-        return lambda start: span_ref[(tile * 2 * group + start // half) // 2 * 2 + me_ref[1]]
+        return lambda start: span_ref[(tile * 2 * group + start // half) // 2 * 2 + my_place]
 
     def both_write(tile, result):
         out_ref[pl.ds(tile * 2 * group, 2 * group), :half, :] = result.reshape(2 * group, half, HD)
@@ -388,7 +400,7 @@
     for block in range(blocks - 2):
         near = near & (span_ref[(block + 2) * block_frames] > span_ref[(block + 1) * block_frames - 1])
     for core, roles in enumerate(((1, own_query, own_span, own_write), (2, both_query, both_span, both_write))):
-        here = me_ref[0] == core
+        here = my_core == core
         pl.when(here & near)(functools.partial(straight, *roles))
         pl.when(here & jnp.logical_not(near))(functools.partial(looped, *roles))
 
@@ -399,22 +411,22 @@
     devices = math.prod(sizes)
     group = BLOCK // rows
     size = group * rows
-    me = jnp.stack([lax.axis_index(axes[0]) % 2, lax.axis_index(axes[1])]).astype(jnp.int32)
-    local, me = lax.optimization_barrier(([array.reshape(rows, width) for array in (queries, keys, values)], me))
+    local = [array.reshape(rows, width) for array in (queries, keys, values)]
     kept = rows - rows // 4
     packed = pl.pallas_call(
         shared_pack_kernel,
         out_shape=pltpu.VMEM((devices, 2 * rows + kept, HD), jnp.bfloat16),
-        in_specs=[VMEM] * 3,
-        out_specs=VMEM,
+        in_specs=[pl.BlockSpec(memory_space=pl.ANY)] * 3,
+        out_specs=VMEM,
+        scratch_shapes=[pltpu.VMEM((3, rows, width), jnp.bfloat16), pltpu.SemaphoreType.DMA((3,))],
     )(*local)
     arrived = lax.all_to_all(packed, axes, split_axis=0, concat_axis=0, tiled=True)
     across = [(device, device ^ sizes[1]) for device in range(devices)]
     rest = lax.ppermute(arrived[:, 2 * rows + rows // 2 :], axes, across)
     result = pl.pallas_call(
-        functools.partial(shared_kernel, (devices, rows, spatial_here, group)),
+        functools.partial(shared_kernel, (devices, rows, spatial_here, group), axes),
         out_shape=pltpu.VMEM((devices, rows, HD), jnp.bfloat16),
-        in_specs=[SMEM, SMEM, VMEM, VMEM],
+        in_specs=[SMEM, VMEM, VMEM],
         out_specs=VMEM,
         scratch_shapes=[
             pltpu.VMEM((2, devices // group, size, size), jnp.float32),
@@ -424,7 +436,6 @@
         ],
     )(
         span_of_frame,
-        me,
         pltpu.with_memory_space_constraint(arrived, pltpu.VMEM),
         pltpu.with_memory_space_constraint(rest, pltpu.VMEM),
     )

time: 70.4 us -> 69.4 us (0.986)
  no operation moved by 1% of the time
where the time goes in v5:
time: 69.4 us; the launch traced here: 69.2 us
  blocking collectives  62.6 us (90%)
  Pallas kernels  5.16 us (7%)
  waiting for transfers between devices  1.33 us (2%)
    all_to_all x1, blocking collectives, shared(): lax.all_to_all(packed, axes, split_axis=0, concat_axis=0, tiled=True)  42.5 us
    all_to_all x1, blocking collectives, shared(): lax.all_to_all(result, axes, split_axis=0, concat_axis=0, tiled=True)  20.1 us
    pallas_call x1, Pallas kernels, shared(): pl.pallas_call(functools.partial(shared_kernel, (devices, rows, spatial_h...  3.02 us
  transfers between devices with their start and end apart: 1, of which 1 were waited for; matrix products, arithmetic and copies ran while one was open for 0% of the time, Pallas kernels for 0%

profile of v5, /device:TPU:1, one launch (start us, length us, event | category | flops | bytes accessed | tf_op | source)
XLA Modules:
  0.0 69.2 jit_solution(13032449108399196219)
XLA Ops:
  0.0 1.3 %shard_map.46 = bf16[32,176,128]{2,1,0:T(8,128)(2,1)S(1)} custom-call(bf16[64,3072]{1,0:T(8,128)(2,1)} %bitcast.4, bf16[64,3072]{1,0:T(8,128)(2,1)} %bitcast.5, bf16[64,3072]{1,0:T(8,128)(2,1)} %bitcast.6), custom_call_target="tpu_custom_call" | custom-call | tf_op jit(solution)/shard_map/pallas_call | solution.py:416
  1.3 42.5 %all_to_all.10.x_ref = bf16[32,176,128]{2,1,0:T(8,128)(2,1)S(1)} all-to-all(bf16[32,176,128]{2,1,0:T(8,128)(2,1)S(1)} %shard_map.46), channel_id=1, replica_groups=mesh['tm'=16,'space'=2] {'tm','space'}, dimensions={0} | all-to-all | bytes 2883584 | tf_op jit(solution)/shard_map/all_to_all | solution.py:423
  43.9 0.1 collective-permute-start
  44.0 1.3 %collective-permute-done.rest_ref = bf16[32,16,128]{2,1,0:T(8,128)(2,1)S(1)} collective-permute-done((bf16[32,16,128]{2,1,0:T(8,128)(2,1)S(1)}, bf16[32,16,128]{2,1,0:T(8,128)(2,1)S(1)}, u32[]{:S(2)}, u32[]{:S(2)}) %collective-permute-start) | collective-permute-done | bytes 131104 | tf_op jit(solution)/shard_map/ppermute | solution.py:425
  45.3 3.0 %shard_map.47 = bf16[32,64,128]{2,1,0:T(8,128)(2,1)S(1)} custom-call(s32[32]{0:T(128)} %span_ref.1, bf16[32,176,128]{2,1,0:T(8,128)(2,1)S(1)} %all_to_all.10.x_ref, bf16[32,16,128]{2,1,0:T(8,128)(2,1)S(1)} %collective-permute-done.rest_ref), custom_call_target="tpu_custom_call" | custom-call | tf_op jit(solution)/shard_map/pallas_call | solution.py:426
  48.3 20.1 %all_to_all.11.in_ref = bf16[32,64,128]{2,1,0:T(8,128)(2,1)S(1)} all-to-all(bf16[32,64,128]{2,1,0:T(8,128)(2,1)S(1)} %shard_map.47), channel_id=1, replica_groups=mesh['tm'=16,'space'=2] {'tm','space'}, dimensions={0} | all-to-all | bytes 1048576 | tf_op jit(solution)/shard_map/all_to_all | solution.py:442
  68.4 0.8 %shard_map.48 = bf16[64,3072]{1,0:T(8,128)(2,1)} custom-call(bf16[32,64,128]{2,1,0:T(8,128)(2,1)S(1)} %all_to_all.11.in_ref), custom_call_target="tpu_custom_call" | custom-call | tf_op jit(solution)/shard_map/pallas_call | solution.py:443
  (1 shorter events, 0.0 us)
Async XLA Ops:
  43.9 1.4 %collective-permute-start = (bf16[32,16,128]{2,1,0:T(8,128)(2,1)S(1)}, bf16[32,16,128]{2,1,0:T(8,128)(2,1)S(1)}, u32[]{:S(2)}, u32[]{:S(2)}) collective-permute-start(bf16[32,16,128]{2,1,0:T(8,128)(2,1)S(1)} %slice.4), channel_id=1, source_target_pairs={{0,2},{1,3},{2,0},{3,1},{4,6},{5,7},{6,4},{7,5},{8,10},{9,11},{10,... | collective-permute-start | bytes 393224 | tf_op jit(solution)/shard_map/ppermute | solution.py:425

commit v6 on v5

--- a/solution.py
+++ b/solution.py
@@ -271,14 +271,22 @@
         out_ref[second, 2 * rows + half :] = of(2, own, kept, rows)
 
 
-def shared_unpack_kernel(in_ref, out_ref):
+def shared_unpack_kernel(in_ref, out_ref, sems):
     rows = out_ref.shape[0]
     half = rows // 2
+    copies = []
     for time in range(0, in_ref.shape[0] // 2, 2):
         for place in range(2):
             own, both = time // 2 * 3 + 2 * place, time // 2 * 3 + 1
-            out_ref[:, own * HD : (own + 1) * HD] = in_ref[time * 2 + place]
-            out_ref[place * half : (place + 1) * half, both * HD : (both + 1) * HD] = in_ref[time * 2 + 2 + place, :half]
+            first, second = time * 2 + place, time * 2 + 2 + place
+            own_out = out_ref.at[:, own * HD : (own + 1) * HD]
+            both_out = out_ref.at[place * half : (place + 1) * half, both * HD : (both + 1) * HD]
+            copies.append(pltpu.make_async_copy(in_ref.at[first], own_out, sems.at[first]))
+            copies.append(pltpu.make_async_copy(in_ref.at[second, :half], both_out, sems.at[second]))
+    for copy in copies:
+        copy.start()
+    for copy in copies:
+        copy.wait()
 
 
 def shared_kernel(plan, axes, span_ref, x_ref, rest_ref, out_ref, score_ref, peak_ref, total_ref, sum_ref):
@@ -444,7 +452,8 @@
         shared_unpack_kernel,
         out_shape=jax.ShapeDtypeStruct((rows, width), jnp.bfloat16),
         in_specs=[VMEM],
-        out_specs=VMEM,
+        out_specs=pl.BlockSpec(memory_space=pl.ANY),
+        scratch_shapes=[pltpu.SemaphoreType.DMA((devices,))],
     )(pltpu.with_memory_space_constraint(returned, pltpu.VMEM))
     return out.reshape(queries.shape)
 

time: 69.4 us -> 69.6 us (level)
  no operation moved by 1% of the time
where the time goes in v6:
time: 69.6 us; the launch traced here: 69.4 us
  blocking collectives  62.6 us (90%)
  Pallas kernels  5.37 us (8%)
  waiting for transfers between devices  1.33 us (2%)
    all_to_all x1, blocking collectives, shared(): lax.all_to_all(packed, axes, split_axis=0, concat_axis=0, tiled=True)  42.5 us
    all_to_all x1, blocking collectives, shared(): lax.all_to_all(result, axes, split_axis=0, concat_axis=0, tiled=True)  20.1 us
    pallas_call x1, Pallas kernels, shared(): pl.pallas_call(functools.partial(shared_kernel, (devices, rows, spatial_h...  3.02 us
  transfers between devices with their start and end apart: 1, of which 1 were waited for; matrix products, arithmetic and copies ran while one was open for 0% of the time, Pallas kernels for 0%

profile of v6, /device:TPU:1, one launch (start us, length us, event | category | flops | bytes accessed | tf_op | source)
XLA Modules:
  0.0 69.4 jit_solution(1566443957136170429)
XLA Ops:
  0.0 1.3 %shard_map.46 = bf16[32,176,128]{2,1,0:T(8,128)(2,1)S(1)} custom-call(bf16[64,3072]{1,0:T(8,128)(2,1)} %bitcast.4, bf16[64,3072]{1,0:T(8,128)(2,1)} %bitcast.5, bf16[64,3072]{1,0:T(8,128)(2,1)} %bitcast.6), custom_call_target="tpu_custom_call" | custom-call | tf_op jit(solution)/shard_map/pallas_call | solution.py:424
  1.3 42.5 %all_to_all.10.x_ref = bf16[32,176,128]{2,1,0:T(8,128)(2,1)S(1)} all-to-all(bf16[32,176,128]{2,1,0:T(8,128)(2,1)S(1)} %shard_map.46), channel_id=1, replica_groups=mesh['tm'=16,'space'=2] {'tm','space'}, dimensions={0} | all-to-all | bytes 2883584 | tf_op jit(solution)/shard_map/all_to_all | solution.py:431
  43.9 0.1 collective-permute-start
  44.0 1.3 %collective-permute-done.rest_ref = bf16[32,16,128]{2,1,0:T(8,128)(2,1)S(1)} collective-permute-done((bf16[32,16,128]{2,1,0:T(8,128)(2,1)S(1)}, bf16[32,16,128]{2,1,0:T(8,128)(2,1)S(1)}, u32[]{:S(2)}, u32[]{:S(2)}) %collective-permute-start) | collective-permute-done | bytes 131104 | tf_op jit(solution)/shard_map/ppermute | solution.py:433
  45.3 3.0 %shard_map.47 = bf16[32,64,128]{2,1,0:T(8,128)(2,1)S(1)} custom-call(s32[32]{0:T(128)} %span_ref.1, bf16[32,176,128]{2,1,0:T(8,128)(2,1)S(1)} %all_to_all.10.x_ref, bf16[32,16,128]{2,1,0:T(8,128)(2,1)S(1)} %collective-permute-done.rest_ref), custom_call_target="tpu_custom_call" | custom-call | tf_op jit(solution)/shard_map/pallas_call | solution.py:434
  48.3 20.1 %all_to_all.11.in_ref = bf16[32,64,128]{2,1,0:T(8,128)(2,1)S(1)} all-to-all(bf16[32,64,128]{2,1,0:T(8,128)(2,1)S(1)} %shard_map.47), channel_id=1, replica_groups=mesh['tm'=16,'space'=2] {'tm','space'}, dimensions={0} | all-to-all | bytes 1048576 | tf_op jit(solution)/shard_map/all_to_all | solution.py:450
  68.4 1.0 %shard_map.48 = bf16[64,3072]{1,0:T(8,128)(2,1)} custom-call(bf16[32,64,128]{2,1,0:T(8,128)(2,1)S(1)} %all_to_all.11.in_ref), custom_call_target="tpu_custom_call" | custom-call | tf_op jit(solution)/shard_map/pallas_call | solution.py:451
  (1 shorter events, 0.0 us)
Async XLA Ops:
  43.9 1.4 %collective-permute-start = (bf16[32,16,128]{2,1,0:T(8,128)(2,1)S(1)}, bf16[32,16,128]{2,1,0:T(8,128)(2,1)S(1)}, u32[]{:S(2)}, u32[]{:S(2)}) collective-permute-start(bf16[32,16,128]{2,1,0:T(8,128)(2,1)S(1)} %slice.4), channel_id=1, source_target_pairs={{0,2},{1,3},{2,0},{3,1},{4,6},{5,7},{6,4},{7,5},{8,10},{9,11},{10,... | collective-permute-start | bytes 393224 | tf_op jit(solution)/shard_map/ppermute | solution.py:433
